TPU v7x, 32 devices: a whole 2x2x4 slice. The times are simulated.
32 devices in a mesh: tm: 2 (over y), rows: 4 (over z), dp: 4 (over x, core).
Axes of the slice: x: 2, y: 2, z: 4, core: 2. Of those that a mesh axis runs over, the one named last changes fastest.
Arguments:
- video: bfloat16 [4, 32, 16, 32, 128], P('dp', 'tm', 'rows'), may hold values from -6 to 6
- cotangent: bfloat16 [4, 32, 16, 32, 128], P('dp', 'tm', 'rows'), may hold values from -6 to 6
- in_kernel: bfloat16 [3, 3, 128, 128], replicated, may hold values from -0.03125 to 0.03125
- out_kernel: bfloat16 [3, 3, 128, 128], replicated, may hold values from -0.1875 to 0.1875
- skip_gain: float32 [128], replicated, may hold values from 0.5 to 1.5
- log_decay: float32 [32, 128], P('tm'), may hold values from -3 to 0, as said below
Outputs:
- layer_out: bfloat16 [4, 32, 16, 32, 128], P('dp', 'tm', 'rows')
- video_grad: bfloat16 [4, 32, 16, 32, 128], P('dp', 'tm', 'rows')
- in_kernel_grad: float32 [3, 3, 128, 128], replicated
- out_kernel_grad: float32 [3, 3, 128, 128], replicated
- skip_gain_grad: float32 [128], replicated
- decay_grad: float32 [32, 128], P('tm')
Inputs may be any that keep to these rules, and one draw needn't show every extreme that they name: log_decay is negative.
All inputs are finite; a program needn't handle non-finite values.
Results may differ from a plain program's by a relative error of at most 0.0085.
Values may be sent and summed in bfloat16 or wider, within the bound.
No kernel may reach another device: no remote copies, remote signals or barrier semaphores. Data moves between devices by JAX's collectives and lax.ppermute only.
A program may use at most 64 MiB of HBM per device.

v0:
```python
import math
import jax
import jax.numpy as jnp
from jax import lax
from jax.sharding import PartitionSpec as P


def padded_2(cells, sides, width):
    for axis, dim in sides:
        count = lax.axis_size(axis)
        ends = count - 1
        head = lax.slice_in_dim(cells, 0, width, axis=dim)
        tail = lax.slice_in_dim(cells, cells.shape[dim] - width, cells.shape[dim], axis=dim)
        cells = jnp.concatenate(
            [
                lax.ppermute(tail, axis, [(i, (i + 1) % count) for i in range(ends)]),
                cells,
                lax.ppermute(head, axis, [((i + 1) % count, i) for i in range(ends)]),
            ],
            axis=dim,
        )
    return cells


def pad_columns(field):
    return jnp.pad(field, ((0, 0), (0, 0), (0, 0), (1, 1), (0, 0)))


def forward_conv(padded, kernel):
    seqs, frames, rows_two, cols_two, chans = padded.shape
    rows, cols = (rows_two - 2, cols_two - 2)
    total = None
    for i in range(3):
        for j in range(3):
            piece = padded[:, :, i : i + rows, j : j + cols, :].reshape(-1, chans)
            term = jnp.dot(piece, kernel[i, j], preferred_element_type=jnp.float32)
            total = term if total is None else total + term
    return total.reshape(seqs, frames, rows, cols, kernel.shape[3])


def adjoint_conv(padded, kernel):
    seqs, frames, rows_two, cols_two, chans = padded.shape
    rows, cols = (rows_two - 2, cols_two - 2)
    total = None
    for i in range(3):
        for j in range(3):
            piece = padded[:, :, 2 - i : 2 - i + rows, 2 - j : 2 - j + cols, :].reshape(-1, chans)
            term = lax.dot_general(
                piece, kernel[i, j], (((1,), (1,)), ((), ())), preferred_element_type=jnp.float32
            )
            total = term if total is None else total + term
    return total.reshape(seqs, frames, rows, cols, kernel.shape[2])


def kernel_grad(padded, grad):
    seqs, frames, rows_two, cols_two, chans = padded.shape
    rows, cols = (rows_two - 2, cols_two - 2)
    flat_grad = grad.reshape(-1, grad.shape[-1])
    outer_list = []
    for i in range(3):
        inner_list = []
        for j in range(3):
            piece = padded[:, :, i : i + rows, j : j + cols, :].reshape(-1, chans)
            inner_list.append(
                lax.dot_general(
                    piece, flat_grad, (((0,), (0,)), ((), ())), preferred_element_type=jnp.float32
                )
            )
        outer_list.append(jnp.stack(inner_list))
    return jnp.stack(outer_list)


def on_device(video, cotangent, in_kernel, out_kernel, skip_gain, log_decay):
    seqs, frames, rows, cols, chans = video.shape
    padded_x = pad_columns(padded_2(video, (("rows", 2),), 1))
    drive = forward_conv(padded_x, in_kernel)
    cum = jnp.cumsum(log_decay, axis=0)
    later_mask = (
        lax.broadcasted_iota(jnp.int32, (frames, frames), 0)
        >= lax.broadcasted_iota(jnp.int32, (frames, frames), 1)
    )[:, :, None]
    gaps = cum[:, None, :] - cum[None, :, :]
    within = jnp.where(later_mask, jnp.exp(jnp.where(later_mask, gaps, 0.0)), 0.0)
    local_states = jnp.einsum("tkp,skrcp->strcp", within, drive, precision=lax.Precision.HIGHEST)
    group_total = cum[-1]
    empty = jnp.zeros_like(local_states[:, -1])
    group_logs = lax.all_gather(group_total[None, :], "tm", axis=0, tiled=True)
    running = jnp.cumsum(group_logs, axis=0)
    own = lax.axis_index("tm")
    own_running = lax.dynamic_index_in_dim(running, own, 0, keepdims=False)
    piece = lax.all_gather(
        local_states[:, -1][None].astype(jnp.bfloat16), "tm", axis=0, tiled=True
    ).astype(jnp.float32)
    count = piece.shape[0]
    upto = running
    index = jnp.arange(count, dtype=jnp.int32)
    reach = own_running[None, :] - group_total[None, :] - upto
    weight = jnp.where((index < own)[:, None], jnp.exp(jnp.minimum(reach, 0.0)), 0.0)
    carry_in = empty + jnp.einsum("np,nsrcp->srcp", weight, piece, precision=lax.Precision.HIGHEST)
    states = local_states + jnp.exp(cum)[None, :, None, None, :] * carry_in[:, None]
    states_bf = states.astype(jnp.bfloat16)
    padded_s = pad_columns(padded_2(states_bf, (("rows", 2),), 1))
    pre = forward_conv(padded_s, out_kernel) + skip_gain * video.astype(jnp.float32)
    activated, pullback = jax.vjp(jax.nn.gelu, pre)
    grad_pre = pullback(cotangent.astype(jnp.float32))[0]
    grad_bf = grad_pre.astype(jnp.bfloat16)
    out_grad = kernel_grad(padded_s, grad_bf)
    gain_grad = jnp.sum(grad_pre * video.astype(jnp.float32), axis=(0, 1, 2, 3))
    padded_g = pad_columns(padded_2(grad_bf, (("rows", 2),), 1))
    state_grad = adjoint_conv(padded_g, out_kernel)
    local_adjoint = jnp.einsum(
        "tkp,strcp->skrcp", within, state_grad, precision=lax.Precision.HIGHEST
    )
    leading = jnp.exp(cum[0])[None, None, None, :] * local_adjoint[:, 0]
    piece = lax.all_gather(leading[None].astype(jnp.bfloat16), "tm", axis=0, tiled=True).astype(
        jnp.float32
    )
    count = piece.shape[0]
    upto = running
    index = jnp.arange(count, dtype=jnp.int32)
    reach = upto - group_logs - own_running[None, :]
    weight = jnp.where((index > own)[:, None], jnp.exp(jnp.minimum(reach, 0.0)), 0.0)
    back_in = empty + jnp.einsum("np,nsrcp->srcp", weight, piece, precision=lax.Precision.HIGHEST)
    adjoint = (
        local_adjoint
        + jnp.exp(group_total[None, :] - cum)[None, :, None, None, :] * back_in[:, None]
    )
    previous = jnp.concatenate([carry_in[:, None], states[:, :-1]], axis=1)
    decay_part = jnp.sum(
        adjoint * jnp.exp(log_decay)[None, :, None, None, :] * previous, axis=(0, 2, 3)
    )
    decay_scale = 1.0 / math.sqrt(seqs * rows * cols * lax.axis_size("rows") * lax.axis_size("dp"))
    decay_grad = lax.psum(decay_part, ("rows", "dp")) * decay_scale
    adjoint_bf = adjoint.astype(jnp.bfloat16)
    in_grad = kernel_grad(padded_x, adjoint_bf)
    padded_a = pad_columns(padded_2(adjoint_bf, (("rows", 2),), 1))
    video_grad = (adjoint_conv(padded_a, in_kernel) + skip_gain * grad_pre).astype(jnp.bfloat16)
    in_sum, out_sum, gain_sum = lax.psum((in_grad, out_grad, gain_grad), ("tm", "rows", "dp"))
    weight_scale = 1.0 / math.sqrt(
        seqs
        * frames
        * rows
        * cols
        * lax.axis_size("tm")
        * lax.axis_size("rows")
        * lax.axis_size("dp")
    )
    return (
        activated.astype(jnp.bfloat16),
        video_grad,
        in_sum * weight_scale,
        out_sum * weight_scale,
        gain_sum * weight_scale,
        decay_grad,
    )


def solution(mesh):
    placed = (
        P("dp", "tm", "rows", None, None),
        P("dp", "tm", "rows", None, None),
        P(),
        P(),
        P(),
        P("tm", None),
    )
    return jax.shard_map(
        on_device,
        mesh=mesh,
        in_specs=placed,
        out_specs=(
            P("dp", "tm", "rows", None, None),
            P("dp", "tm", "rows", None, None),
            P(),
            P(),
            P(),
            P("tm", None),
        ),
        check_vma=False,
    )
```

profile of v0, /device:TPU:0, one launch (start us, length us, event | category | flops | bytes accessed | tf_op | source)
XLA Modules:
  0.0 367.8 jit_solution(14901978521855251328)
XLA Ops:
  7.2 1.0 fusion.177
  8.2 5.0 %collective-permute-start = (bf16[1,16,1,32,128]{4,3,2,1,0:T(8,128)(2,1)S(1)}, bf16[1,16,1,32,128]{4,3,2,1,0:T(8,128)(2,1)S(1)}, u32[]{:S(2)}, u32[]{:S(2)}) collective-permute-start(bf16[1,16,1,32,128]{4,3,2,1,0:T(8,128)(2,1)S(1)} %get-tuple-element.71), channel_id=1, source_target_pairs={{0,4},{4,8},{8,12},{1,5},{5,9},{9,13},{2,6},{6,10},{10,14},{3,7},{... | collective-permute-start | bytes 393224 | tf_op jit(solution)/shard_map/ppermute | solution.py:16
  13.2 1.3 collective-permute-start.1
  14.5 0.7 reduce_window_sum.22
  15.2 4.2 %all-gather = f32[2,1,128]{2,1,0:T(1,128)S(1)} all-gather(f32[1,1,128]{2,1,0:T(1,128)S(1)} %slice_bitcast_fusion.1), channel_id=1, replica_groups=mesh['tm'=2,'rows'=4,'dp'=4] {'tm'}, dimensions={0}, use_global_device_ids=true | all-gather | bytes 1536 | tf_op jit(solution)/shard_map/all_gather | solution.py:87
  20.0 1.6 fusion.25
  21.7 0.6 fusion.173
  25.6 4.5 %copy.169 = f32[16,4,32,128]{2,0,1,3:T(8,128)} copy(f32[16,4,32,128]{3,2,1,0:T(8,128)S(1)} %bitcast.443) | data formatting | bytes 2097152 | tf_op jit(solution)/shard_map/reshape
  30.1 8.3 %fusion.19 = f32[128,4,32,16]{2,3,1,0:T(8,128)} fusion(f32[16,4,32,128]{2,0,1,3:T(8,128)} %copy.169, f32[16,128]{0,1:T(8,128)S(1)} %copy.167, pred[16,16]{0,1:T(8,128)(4,1)S(1)} %iota_compare_fusion.2), kind=kOutput, calls=%fused_computation.74 | convolution fusion | flops 50429952 | bytes 2105600 | tf_op jit(solution)/shard_map/tkp,skrcp->strcp/dot_general | solution.py:84
  38.4 3.7 %copy.171 = f32[128,4,32,16]{0,2,1,3:T(8,128)S(1)} copy(f32[128,4,32,16]{2,3,1,0:T(8,128)} %fusion.19) | data formatting | bytes 2097152 | tf_op jit(solution)/shard_map/tkp,skrcp->strcp/dot_general | solution.py:84
  42.1 4.6 %all_gather.9 = bf16[2,1,4,32,128]{4,3,2,1,0:T(8,128)(2,1)S(1)} all-gather(bf16[1,1,4,32,128]{4,3,2,1,0:T(8,128)(2,1)S(1)} %slice.550), channel_id=1, replica_groups=mesh['tm'=2,'rows'=4,'dp'=4] {'tm'}, dimensions={0}, use_global_device_ids=true | all-gather | bytes 98304 | tf_op jit(solution)/shard_map/all_gather | solution.py:91
  47.0 4.2 %collective-permute-start.2 = (bf16[1,16,1,32,128]{4,3,2,1,0:T(8,128)(2,1)S(1)}, bf16[1,16,1,32,128]{4,3,2,1,0:T(8,128)(2,1)S(1)}, u32[]{:S(2)}, u32[]{:S(2)}) collective-permute-start(bf16[1,16,1,32,128]{4,3,2,1,0:T(8,128)(2,1)S(1)} %get-tuple-element.67), channel_id=1, source_target_pairs={{0,4},{4,8},{8,12},{1,5},{5,9},{9,13},{2,6},{6,10},{10,14},{3,7},{... | collective-permute-start | bytes 393224 | tf_op jit(solution)/shard_map/ppermute | solution.py:16
  51.2 1.5 collective-permute-start.3
  52.7 1.1 slice.347
  53.9 4.2 %collective-permute-done.3 = bf16[1,16,1,32,128]{4,3,2,1,0:T(8,128)(2,1)S(1)} collective-permute-done((bf16[1,16,1,32,128]{4,3,2,1,0:T(8,128)(2,1)S(1)}, bf16[1,16,1,32,128]{4,3,2,1,0:T(8,128)(2,1)S(1)}, u32[]{:S(2)}, u32[]{:S(2)}) %collective-permute-start.3) | collective-permute-done | bytes 131104 | tf_op jit(solution)/shard_map/ppermute | solution.py:18
  58.1 0.5 select_maximum_fusion.4
  58.6 0.6 fusion.172
  62.2 0.7 copy-done.8
  62.9 1.8 fusion.6
  64.8 1.0 convolution_bitcast_fusion.4
  65.8 1.0 convolution_bitcast_fusion.1
  66.7 1.0 convolution_bitcast_fusion.7
  67.7 1.0 convolution_bitcast_fusion.5
  68.7 1.0 convolution_bitcast_fusion.3
  69.7 1.0 convolution_bitcast_fusion.2
  70.6 1.0 convolution_bitcast_fusion
  71.6 1.0 convolution_bitcast_fusion.8
  72.5 1.0 convolution_bitcast_fusion.6
  73.5 0.7 fusion.175
  74.2 40.4 %psum.30 = f32[128]{0:T(128)S(1)} all-reduce(f32[128]{0:T(128)S(1)} %get-tuple-element.26), channel_id=1, replica_groups=mesh['tm'=2,'rows'=4,'dp'=4] {'tm','rows','dp'}, use_global_device_ids=true, to_apply=%region_5.6 | all-reduce | flops 128 | bytes 1024 | tf_op jit(solution)/shard_map/psum | solution.py:138
  114.6 0.5 broadcast_multiply_fusion.3
  115.1 2.2 collective-permute-start.4
  117.3 1.5 collective-permute-start.5
  118.8 0.9 maximum_bitcast_fusion.4
  119.7 0.9 maximum_bitcast_fusion.5
  120.6 0.9 maximum_bitcast_fusion.3
  121.6 0.9 pad_maximum_fusion.1
  122.4 1.9 collective-permute-done.5
  124.8 0.6 fusion.171
  127.9 1.3 fusion.1
  129.2 5.4 %copy.172 = f32[16,4,32,128]{2,0,1,3:T(8,128)} copy(f32[16,4,32,128]{3,2,1,0:T(8,128)} %bitcast.442) | data formatting | bytes 2097152 | tf_op jit(solution)/shard_map/reshape.7
  134.6 8.1 %fusion.17 = f32[128,4,32,16]{2,3,1,0:T(8,128)} fusion(f32[16,4,32,128]{2,0,1,3:T(8,128)} %copy.172, f32[16,128]{0,1:T(8,128)S(1)} %copy.167, pred[16,16]{0,1:T(8,128)(4,1)S(1)} %iota_compare_fusion.2), kind=kOutput, calls=%fused_computation.72 | convolution fusion | flops 50429952 | bytes 2105600 | tf_op jit(solution)/shard_map/tkp,strcp->skrcp/dot_general | solution.py:111
  142.8 4.5 %copy.173 = f32[128,4,32,16]{0,2,1,3:T(8,128)} copy(f32[128,4,32,16]{2,3,1,0:T(8,128)} %fusion.17) | data formatting | bytes 2097152 | tf_op jit(solution)/shard_map/tkp,strcp->skrcp/dot_general | solution.py:111
  147.3 0.9 fusion.71
  148.2 5.1 %all_gather.11 = bf16[2,1,4,32,128]{4,3,2,1,0:T(8,128)(2,1)S(1)} all-gather(bf16[1,1,4,32,128]{4,3,2,1,0:T(8,128)(2,1)S(1)} %fusion.71), channel_id=1, replica_groups=mesh['tm'=2,'rows'=4,'dp'=4] {'tm'}, dimensions={0}, use_global_device_ids=true | all-gather | bytes 98304 | tf_op jit(solution)/shard_map/all_gather | solution.py:115
  153.3 1.9 fusion.16
  155.9 1.0 convolution_bitcast_fusion.14
  157.6 1.0 convolution_bitcast_fusion.11
  158.6 1.0 convolution_bitcast_fusion.9
  159.5 1.0 convolution_bitcast_fusion.17
  160.5 1.0 convolution_bitcast_fusion.15
  161.6 57.8 %psum.31 = f32[16,128]{0,1:T(8,128)S(1)} all-reduce(f32[16,128]{0,1:T(8,128)S(1)} %copy.212), channel_id=1, replica_groups=mesh['tm'=2,'rows'=4,'dp'=4] {'rows','dp'}, use_global_device_ids=true, to_apply=%region_7.8 | all-reduce | flops 2048 | bytes 16384 | tf_op jit(solution)/shard_map/psum | solution.py:133
  219.4 1.3 collective-permute-start.6
  220.7 1.3 collective-permute-start.7
  222.0 0.9 maximum_bitcast_fusion.2
  222.9 0.9 maximum_bitcast_fusion
  223.8 0.7 copy.176
  224.5 0.9 pad_maximum_fusion
  225.4 2.2 collective-permute-done.7
  228.1 0.6 fusion.170
  231.8 1.0 add_convert_fusion
  232.8 124.3 %all-reduce.7.cloned.1.call-done = (f32[3,3,128,128]{3,2,1,0:T(8,128)}, f32[3,3,128,128]{3,2,1,0:T(8,128)}) async-done(((f32[3,3,128,128]{3,2,1,0:T(8,128)}, f32[3,3,128,128]{3,2,1,0:T(8,128)}), (f32[3,3,128,128]{3,2,1,0:T(8,128)}, f32[3,3,128,128]{3,2,1,0:T(8,128)})) %all-reduce.7.cloned.1.call-update) | async-done | bytes 1179664 | tf_op jit(solution)/shard_map/psum | solution.py:138
  357.2 1.9 broadcast_multiply_fusion.1
  359.1 1.9 broadcast_multiply_fusion
  (94 shorter events, 15.3 us)
Async XLA Ops:
  7.2 350.0 %all-reduce.7.cloned.1.call-start = ((), (), s32[]{:S(2)}) async-start(), calls=%async_computation | async-start | bytes 2359296 | tf_op jit(solution)/shard_map/psum | solution.py:138
  8.2 11.5 %collective-permute-start = (bf16[1,16,1,32,128]{4,3,2,1,0:T(8,128)(2,1)S(1)}, bf16[1,16,1,32,128]{4,3,2,1,0:T(8,128)(2,1)S(1)}, u32[]{:S(2)}, u32[]{:S(2)}) collective-permute-start(bf16[1,16,1,32,128]{4,3,2,1,0:T(8,128)(2,1)S(1)} %get-tuple-element.71), channel_id=1, source_target_pairs={{0,4},{4,8},{8,12},{1,5},{5,9},{9,13},{2,6},{6,10},{10,14},{3,7},{... | collective-permute-start | bytes 393224 | tf_op jit(solution)/shard_map/ppermute | solution.py:16
  13.2 6.9 %collective-permute-start.1 = (bf16[1,16,1,32,128]{4,3,2,1,0:T(8,128)(2,1)S(1)}, bf16[1,16,1,32,128]{4,3,2,1,0:T(8,128)(2,1)S(1)}, u32[]{:S(2)}, u32[]{:S(2)}) collective-permute-start(bf16[1,16,1,32,128]{4,3,2,1,0:T(8,128)(2,1)S(1)} %get-tuple-element.72), channel_id=1, source_target_pairs={{4,0},{8,4},{12,8},{5,1},{9,5},{13,9},{6,2},{10,6},{14,10},{7,3},{... | collective-permute-start | bytes 393224 | tf_op jit(solution)/shard_map/ppermute | solution.py:18
  21.7 1.0 copy-start.6
  22.3 1.1 copy-start
  23.4 0.8 copy-start.3
  23.4 1.9 copy-start.1
  42.1 10.6 %copy-start.10 = (f32[16,128]{1,0:T(8,128)S(1)}, f32[16,128]{1,0:T(8,128)}, u32[]{:S(2)}) copy-start(f32[16,128]{1,0:T(8,128)} %param.11) | copy-start | bytes 24580
  47.0 6.9 %collective-permute-start.2 = (bf16[1,16,1,32,128]{4,3,2,1,0:T(8,128)(2,1)S(1)}, bf16[1,16,1,32,128]{4,3,2,1,0:T(8,128)(2,1)S(1)}, u32[]{:S(2)}, u32[]{:S(2)}) collective-permute-start(bf16[1,16,1,32,128]{4,3,2,1,0:T(8,128)(2,1)S(1)} %get-tuple-element.67), channel_id=1, source_target_pairs={{0,4},{4,8},{8,12},{1,5},{5,9},{9,13},{2,6},{6,10},{10,14},{3,7},{... | collective-permute-start | bytes 393224 | tf_op jit(solution)/shard_map/ppermute | solution.py:16
  51.2 6.9 %collective-permute-start.3 = (bf16[1,16,1,32,128]{4,3,2,1,0:T(8,128)(2,1)S(1)}, bf16[1,16,1,32,128]{4,3,2,1,0:T(8,128)(2,1)S(1)}, u32[]{:S(2)}, u32[]{:S(2)}) collective-permute-start(bf16[1,16,1,32,128]{4,3,2,1,0:T(8,128)(2,1)S(1)} %get-tuple-element.68), channel_id=1, source_target_pairs={{4,0},{8,4},{12,8},{5,1},{9,5},{13,9},{6,2},{10,6},{14,10},{7,3},{... | collective-permute-start | bytes 393224 | tf_op jit(solution)/shard_map/ppermute | solution.py:18
  58.6 1.0 copy-start.5
  61.9 1.0 copy-start.8
  61.9 1.0 copy-start.11
  115.1 7.3 %collective-permute-start.4 = (bf16[1,16,1,32,128]{4,3,2,1,0:T(8,128)(2,1)}, bf16[1,16,1,32,128]{4,3,2,1,0:T(8,128)(2,1)S(1)}, u32[]{:S(2)}, u32[]{:S(2)}) collective-permute-start(bf16[1,16,1,32,128]{4,3,2,1,0:T(8,128)(2,1)} %get-tuple-element.63), channel_id=1, source_target_pairs={{0,4},{4,8},{8,12},{1,5},{5,9},{9,13},{2,6},{6,10},{10,14},{3,7},{... | collective-permute-start | bytes 393224 | tf_op jit(solution)/shard_map/ppermute | solution.py:16
  117.3 7.1 %collective-permute-start.5 = (bf16[1,16,1,32,128]{4,3,2,1,0:T(8,128)(2,1)}, bf16[1,16,1,32,128]{4,3,2,1,0:T(8,128)(2,1)S(1)}, u32[]{:S(2)}, u32[]{:S(2)}) collective-permute-start(bf16[1,16,1,32,128]{4,3,2,1,0:T(8,128)(2,1)} %get-tuple-element.64), channel_id=1, source_target_pairs={{4,0},{8,4},{12,8},{5,1},{9,5},{13,9},{6,2},{10,6},{14,10},{7,3},{... | collective-permute-start | bytes 393224 | tf_op jit(solution)/shard_map/ppermute | solution.py:18
  147.3 7.9 %copy-start.2 = (bf16[1,16,4,32,128]{4,3,2,1,0:T(8,128)(2,1)S(1)}, bf16[1,16,4,32,128]{4,3,2,1,0:T(8,128)(2,1)}, u32[]{:S(2)}) copy-start(bf16[1,16,4,32,128]{4,3,2,1,0:T(8,128)(2,1)} %copy-done.1) | copy-start | bytes 1572868
  153.3 2.3 copy-start.4
  160.5 61.5 %copy-start.9 = (f32[1,128,128]{2,1,0:T(8,128)S(1)}, f32[1,128,128]{2,1,0:T(8,128)}, u32[]{:S(2)}) copy-start(f32[1,128,128]{2,1,0:T(8,128)} %convolution_bitcast_fusion.14) | copy-start | bytes 196612
  219.4 6.0 %collective-permute-start.6 = (bf16[1,16,1,32,128]{4,3,2,1,0:T(8,128)(2,1)S(1)}, bf16[1,16,1,32,128]{4,3,2,1,0:T(8,128)(2,1)S(1)}, u32[]{:S(2)}, u32[]{:S(2)}) collective-permute-start(bf16[1,16,1,32,128]{4,3,2,1,0:T(8,128)(2,1)S(1)} %get-tuple-element.59), channel_id=1, source_target_pairs={{0,4},{4,8},{8,12},{1,5},{5,9},{9,13},{2,6},{6,10},{10,14},{3,7},{... | collective-permute-start | bytes 393224 | tf_op jit(solution)/shard_map/ppermute | solution.py:16
  220.7 6.9 %collective-permute-start.7 = (bf16[1,16,1,32,128]{4,3,2,1,0:T(8,128)(2,1)S(1)}, bf16[1,16,1,32,128]{4,3,2,1,0:T(8,128)(2,1)S(1)}, u32[]{:S(2)}, u32[]{:S(2)}) collective-permute-start(bf16[1,16,1,32,128]{4,3,2,1,0:T(8,128)(2,1)S(1)} %get-tuple-element.60), channel_id=1, source_target_pairs={{4,0},{8,4},{12,8},{5,1},{9,5},{13,9},{6,2},{10,6},{14,10},{7,3},{... | collective-permute-start | bytes 393224 | tf_op jit(solution)/shard_map/ppermute | solution.py:18
  228.0 1.0 copy-start.7
Sparse Core Ops, SparseCore 0:
  225.5 131.6 all-reduce.6
where the time goes:
time: 369 us; the launch traced here: 368 us
  waiting for transfers between devices  133 us (36%)
  blocking collectives  112 us (30%)
  matrix products  42.6 us (12%)
  local copies, waits for them, and re-layouts  26.5 us (7%)
  other arithmetic  20.8 us (6%)
  starting transfers between devices  18.3 us (5%)
  between operations  14.6 us (4%)
    psum x1, waiting for transfers between devices, on_device(): lax.psum((in_grad, out_grad, gain_grad), ('tm', 'rows', 'dp'))  124 us
    psum x1, blocking collectives, on_device(): decay_grad = lax.psum(decay_part, ('rows', 'dp')) * decay_scale  57.8 us
    psum x1, blocking collectives, on_device(): lax.psum((in_grad, out_grad, gain_grad), ('tm', 'rows', 'dp'))  40.4 us
    dot_general x18, matrix products, kernel_grad(): lax.dot_general(piece, flat_grad, (((0,), (0,)), ((), ())), preferred_ele...  14.9 us
    ppermute x4, starting transfers between devices, padded_2(): lax.ppermute(tail, axis, [(i, (i + 1) % count) for i in range(ends)])  12.7 us
    ppermute x4, waiting for transfers between devices, padded_2(): lax.ppermute(head, axis, [((i + 1) % count, i) for i in range(ends)])  8.64 us
    dot_general x1, matrix products, on_device(): jnp.einsum('tkp,skrcp->strcp', within, drive, precision=lax.Precision.HIG...  8.27 us
    dot_general x1, matrix products, on_device(): jnp.einsum('tkp,strcp->skrcp', within, state_grad, precision=lax.Precisio...  8.14 us
  transfers between devices with their start and end apart: 9, of which 5 were waited for; matrix products, arithmetic and copies ran while one was open for 4% of the time, Pallas kernels for 0%

commit v1 on v0

--- a/solution.py
+++ b/solution.py
@@ -130,7 +130,7 @@
         adjoint * jnp.exp(log_decay)[None, :, None, None, :] * previous, axis=(0, 2, 3)
     )
     decay_scale = 1.0 / math.sqrt(seqs * rows * cols * lax.axis_size("rows") * lax.axis_size("dp"))
-    decay_grad = lax.psum(decay_part, ("rows", "dp")) * decay_scale
+    decay_grad = jnp.sum(lax.all_gather(decay_part, ("rows", "dp")), axis=0) * decay_scale
     adjoint_bf = adjoint.astype(jnp.bfloat16)
     in_grad = kernel_grad(padded_x, adjoint_bf)
     padded_a = pad_columns(padded_2(adjoint_bf, (("rows", 2),), 1))

time: 369 us -> 331 us (0.90)
  blocking collectives: 112 us -> 75.9 us
    psum x1 -> x0, blocking collectives: 57.8 us -> none  [on_device(): decay_grad = lax.psum(decay_part, ('rows', 'dp')) * decay_scale]
    all_gather x0 -> x1, blocking collectives: none -> 21.7 us  [on_device(): lax.all_gather(decay_part, ('rows', 'dp'))]
where the time goes in v1:
time: 331 us; the launch traced here: 330 us
  waiting for transfers between devices  131 us (40%)
  blocking collectives  75.9 us (23%)
  matrix products  42.6 us (13%)
  local copies, waits for them, and re-layouts  25.7 us (8%)
  other arithmetic  21.4 us (6%)
  starting transfers between devices  18.3 us (6%)
  between operations  14.6 us (4%)
    psum x1, waiting for transfers between devices, on_device(): lax.psum((in_grad, out_grad, gain_grad), ('tm', 'rows', 'dp'))  122 us
    psum x1, blocking collectives, on_device(): lax.psum((in_grad, out_grad, gain_grad), ('tm', 'rows', 'dp'))  40.4 us
    all_gather x1, blocking collectives, on_device(): lax.all_gather(decay_part, ('rows', 'dp'))  21.7 us
    dot_general x18, matrix products, kernel_grad(): lax.dot_general(piece, flat_grad, (((0,), (0,)), ((), ())), preferred_ele...  14.9 us
    ppermute x4, starting transfers between devices, padded_2(): lax.ppermute(tail, axis, [(i, (i + 1) % count) for i in range(ends)])  12.7 us
    ppermute x4, waiting for transfers between devices, padded_2(): lax.ppermute(head, axis, [((i + 1) % count, i) for i in range(ends)])  9.49 us
    dot_general x1, matrix products, on_device(): jnp.einsum('tkp,skrcp->strcp', within, drive, precision=lax.Precision.HIG...  8.27 us
    dot_general x1, matrix products, on_device(): jnp.einsum('tkp,strcp->skrcp', within, state_grad, precision=lax.Precisio...  8.14 us
  transfers between devices with their start and end apart: 9, of which 5 were waited for; matrix products, arithmetic and copies ran while one was open for 4% of the time, Pallas kernels for 0%

profile of v1, /device:TPU:0, one launch (start us, length us, event | category | flops | bytes accessed | tf_op | source)
XLA Modules:
  0.0 329.6 jit_solution(17517662137105779410)
XLA Ops:
  7.2 1.0 fusion.177
  8.2 5.0 %collective-permute-start = (bf16[1,16,1,32,128]{4,3,2,1,0:T(8,128)(2,1)S(1)}, bf16[1,16,1,32,128]{4,3,2,1,0:T(8,128)(2,1)S(1)}, u32[]{:S(2)}, u32[]{:S(2)}) collective-permute-start(bf16[1,16,1,32,128]{4,3,2,1,0:T(8,128)(2,1)S(1)} %get-tuple-element.53), channel_id=1, source_target_pairs={{0,4},{4,8},{8,12},{1,5},{5,9},{9,13},{2,6},{6,10},{10,14},{3,7},{... | collective-permute-start | bytes 393224 | tf_op jit(solution)/shard_map/ppermute | solution.py:16
  13.2 1.3 collective-permute-start.1
  14.5 0.7 reduce_window_sum.22
  15.2 4.2 %all-gather.1 = f32[2,1,128]{2,1,0:T(1,128)S(1)} all-gather(f32[1,1,128]{2,1,0:T(1,128)S(1)} %slice_bitcast_fusion.1), channel_id=1, replica_groups=mesh['tm'=2,'rows'=4,'dp'=4] {'tm'}, dimensions={0}, use_global_device_ids=true | all-gather | bytes 1536 | tf_op jit(solution)/shard_map/all_gather | solution.py:87
  20.0 1.6 fusion.25
  21.7 0.6 fusion.173
  25.6 4.5 %copy.250 = f32[16,4,32,128]{2,0,1,3:T(8,128)} copy(f32[16,4,32,128]{3,2,1,0:T(8,128)S(1)} %bitcast.444) | data formatting | bytes 2097152 | tf_op jit(solution)/shard_map/reshape
  30.1 8.3 %fusion.19 = f32[128,4,32,16]{2,3,1,0:T(8,128)} fusion(f32[16,4,32,128]{2,0,1,3:T(8,128)} %copy.250, f32[16,128]{0,1:T(8,128)S(1)} %copy.248, pred[16,16]{0,1:T(8,128)(4,1)S(1)} %iota_compare_fusion.2), kind=kOutput, calls=%fused_computation.74 | convolution fusion | flops 50429952 | bytes 2105600 | tf_op jit(solution)/shard_map/tkp,skrcp->strcp/dot_general | solution.py:84
  38.4 3.7 %copy.252 = f32[128,4,32,16]{0,2,1,3:T(8,128)S(1)} copy(f32[128,4,32,16]{2,3,1,0:T(8,128)} %fusion.19) | data formatting | bytes 2097152 | tf_op jit(solution)/shard_map/tkp,skrcp->strcp/dot_general | solution.py:84
  42.1 4.6 %all_gather.15 = bf16[2,1,4,32,128]{4,3,2,1,0:T(8,128)(2,1)S(1)} all-gather(bf16[1,1,4,32,128]{4,3,2,1,0:T(8,128)(2,1)S(1)} %slice.550), channel_id=1, replica_groups=mesh['tm'=2,'rows'=4,'dp'=4] {'tm'}, dimensions={0}, use_global_device_ids=true | all-gather | bytes 98304 | tf_op jit(solution)/shard_map/all_gather | solution.py:91
  47.0 4.2 %collective-permute-start.2 = (bf16[1,16,1,32,128]{4,3,2,1,0:T(8,128)(2,1)S(1)}, bf16[1,16,1,32,128]{4,3,2,1,0:T(8,128)(2,1)S(1)}, u32[]{:S(2)}, u32[]{:S(2)}) collective-permute-start(bf16[1,16,1,32,128]{4,3,2,1,0:T(8,128)(2,1)S(1)} %get-tuple-element.49), channel_id=1, source_target_pairs={{0,4},{4,8},{8,12},{1,5},{5,9},{9,13},{2,6},{6,10},{10,14},{3,7},{... | collective-permute-start | bytes 393224 | tf_op jit(solution)/shard_map/ppermute | solution.py:16
  51.2 1.5 collective-permute-start.3
  52.7 1.1 slice.347
  53.9 4.2 %collective-permute-done.3 = bf16[1,16,1,32,128]{4,3,2,1,0:T(8,128)(2,1)S(1)} collective-permute-done((bf16[1,16,1,32,128]{4,3,2,1,0:T(8,128)(2,1)S(1)}, bf16[1,16,1,32,128]{4,3,2,1,0:T(8,128)(2,1)S(1)}, u32[]{:S(2)}, u32[]{:S(2)}) %collective-permute-start.3) | collective-permute-done | bytes 131104 | tf_op jit(solution)/shard_map/ppermute | solution.py:18
  58.1 0.5 select_maximum_fusion.4
  58.6 0.6 fusion.172
  62.2 0.7 copy-done.8
  62.9 1.8 fusion.6
  64.8 1.0 convolution_bitcast_fusion.4
  65.8 1.0 convolution_bitcast_fusion.1
  66.7 1.0 convolution_bitcast_fusion.7
  67.7 1.0 convolution_bitcast_fusion.5
  68.7 1.0 convolution_bitcast_fusion.3
  69.7 1.0 convolution_bitcast_fusion.2
  70.6 1.0 convolution_bitcast_fusion
  71.6 1.0 convolution_bitcast_fusion.8
  72.5 1.0 convolution_bitcast_fusion.6
  73.5 0.7 fusion.175
  74.2 40.4 %psum.23 = f32[128]{0:T(128)S(1)} all-reduce(f32[128]{0:T(128)S(1)} %get-tuple-element.8), channel_id=1, replica_groups=mesh['tm'=2,'rows'=4,'dp'=4] {'tm','rows','dp'}, use_global_device_ids=true, to_apply=%region_5.6 | all-reduce | flops 128 | bytes 1024 | tf_op jit(solution)/shard_map/psum | solution.py:138
  114.6 0.5 broadcast_multiply_fusion.3
  115.1 2.2 collective-permute-start.4
  117.3 1.5 collective-permute-start.5
  118.8 0.9 maximum_bitcast_fusion.4
  119.7 0.9 maximum_bitcast_fusion.5
  120.6 0.9 maximum_bitcast_fusion.3
  121.6 0.9 pad_maximum_fusion.1
  122.4 1.9 collective-permute-done.5
  124.8 0.6 fusion.171
  127.9 1.3 fusion.1
  129.2 5.4 %copy.253 = f32[16,4,32,128]{2,0,1,3:T(8,128)} copy(f32[16,4,32,128]{3,2,1,0:T(8,128)} %bitcast.443) | data formatting | bytes 2097152 | tf_op jit(solution)/shard_map/reshape.7
  134.6 8.1 %fusion.17 = f32[128,4,32,16]{2,3,1,0:T(8,128)} fusion(f32[16,4,32,128]{2,0,1,3:T(8,128)} %copy.253, f32[16,128]{0,1:T(8,128)S(1)} %copy.248, pred[16,16]{0,1:T(8,128)(4,1)S(1)} %iota_compare_fusion.2), kind=kOutput, calls=%fused_computation.72 | convolution fusion | flops 50429952 | bytes 2105600 | tf_op jit(solution)/shard_map/tkp,strcp->skrcp/dot_general | solution.py:111
  142.8 4.5 %copy.254 = f32[128,4,32,16]{0,2,1,3:T(8,128)} copy(f32[128,4,32,16]{2,3,1,0:T(8,128)} %fusion.17) | data formatting | bytes 2097152 | tf_op jit(solution)/shard_map/tkp,strcp->skrcp/dot_general | solution.py:111
  147.3 0.9 fusion.71
  148.2 5.1 %all_gather.17 = bf16[2,1,4,32,128]{4,3,2,1,0:T(8,128)(2,1)S(1)} all-gather(bf16[1,1,4,32,128]{4,3,2,1,0:T(8,128)(2,1)S(1)} %fusion.71), channel_id=1, replica_groups=mesh['tm'=2,'rows'=4,'dp'=4] {'tm'}, dimensions={0}, use_global_device_ids=true | all-gather | bytes 98304 | tf_op jit(solution)/shard_map/all_gather | solution.py:115
  153.3 1.9 fusion.16
  155.9 1.0 convolution_bitcast_fusion.14
  157.6 1.0 convolution_bitcast_fusion.11
  158.6 1.0 convolution_bitcast_fusion.9
  159.5 1.0 convolution_bitcast_fusion.17
  160.5 1.0 convolution_bitcast_fusion.15
  161.5 21.7 %all-gather = f32[256,128]{1,0:T(8,128)S(1)} all-gather(f32[16,128]{1,0:T(8,128)S(1)} %get-tuple-element.13), channel_id=2, replica_groups=mesh['tm'=2,'rows'=4,'dp'=4] {'rows','dp'}, dimensions={0}, use_global_device_ids=true | all-gather | bytes 139264 | tf_op jit(solution)/shard_map/all_gather | solution.py:133
  183.2 1.3 collective-permute-start.6
  184.5 1.3 collective-permute-start.7
  185.8 0.9 maximum_bitcast_fusion.2
  186.7 0.9 maximum_bitcast_fusion
  187.6 0.9 pad_maximum_fusion
  188.5 0.6 broadcast_multiply_fusion.2
  189.1 3.0 collective-permute-done.7
  192.6 0.6 fusion.170
  196.3 1.0 add_convert_fusion
  197.4 121.6 %all-reduce.7.cloned.1.call-done = (f32[3,3,128,128]{3,2,1,0:T(8,128)}, f32[3,3,128,128]{3,2,1,0:T(8,128)}) async-done(((f32[3,3,128,128]{3,2,1,0:T(8,128)}, f32[3,3,128,128]{3,2,1,0:T(8,128)}), (f32[3,3,128,128]{3,2,1,0:T(8,128)}, f32[3,3,128,128]{3,2,1,0:T(8,128)})) %all-reduce.7.cloned.1.call-update) | async-done | bytes 1179664 | tf_op jit(solution)/shard_map/psum | solution.py:138
  319.0 1.9 broadcast_multiply_fusion.1
  320.9 1.9 broadcast_multiply_fusion
  (93 shorter events, 15.2 us)
Async XLA Ops:
  7.2 311.8 %all-reduce.7.cloned.1.call-start = ((), (), s32[]{:S(2)}) async-start(), calls=%async_computation | async-start | bytes 2359296 | tf_op jit(solution)/shard_map/psum | solution.py:138
  8.2 11.5 %collective-permute-start = (bf16[1,16,1,32,128]{4,3,2,1,0:T(8,128)(2,1)S(1)}, bf16[1,16,1,32,128]{4,3,2,1,0:T(8,128)(2,1)S(1)}, u32[]{:S(2)}, u32[]{:S(2)}) collective-permute-start(bf16[1,16,1,32,128]{4,3,2,1,0:T(8,128)(2,1)S(1)} %get-tuple-element.53), channel_id=1, source_target_pairs={{0,4},{4,8},{8,12},{1,5},{5,9},{9,13},{2,6},{6,10},{10,14},{3,7},{... | collective-permute-start | bytes 393224 | tf_op jit(solution)/shard_map/ppermute | solution.py:16
  13.2 6.9 %collective-permute-start.1 = (bf16[1,16,1,32,128]{4,3,2,1,0:T(8,128)(2,1)S(1)}, bf16[1,16,1,32,128]{4,3,2,1,0:T(8,128)(2,1)S(1)}, u32[]{:S(2)}, u32[]{:S(2)}) collective-permute-start(bf16[1,16,1,32,128]{4,3,2,1,0:T(8,128)(2,1)S(1)} %get-tuple-element.54), channel_id=1, source_target_pairs={{4,0},{8,4},{12,8},{5,1},{9,5},{13,9},{6,2},{10,6},{14,10},{7,3},{... | collective-permute-start | bytes 393224 | tf_op jit(solution)/shard_map/ppermute | solution.py:18
  21.7 1.0 copy-start.6
  22.3 1.1 copy-start
  23.4 0.8 copy-start.3
  23.4 1.9 copy-start.1
  42.1 10.6 %copy-start.10 = (f32[16,128]{1,0:T(8,128)S(1)}, f32[16,128]{1,0:T(8,128)}, u32[]{:S(2)}) copy-start(f32[16,128]{1,0:T(8,128)} %param.11) | copy-start | bytes 24580
  47.0 6.9 %collective-permute-start.2 = (bf16[1,16,1,32,128]{4,3,2,1,0:T(8,128)(2,1)S(1)}, bf16[1,16,1,32,128]{4,3,2,1,0:T(8,128)(2,1)S(1)}, u32[]{:S(2)}, u32[]{:S(2)}) collective-permute-start(bf16[1,16,1,32,128]{4,3,2,1,0:T(8,128)(2,1)S(1)} %get-tuple-element.49), channel_id=1, source_target_pairs={{0,4},{4,8},{8,12},{1,5},{5,9},{9,13},{2,6},{6,10},{10,14},{3,7},{... | collective-permute-start | bytes 393224 | tf_op jit(solution)/shard_map/ppermute | solution.py:16
  51.2 6.9 %collective-permute-start.3 = (bf16[1,16,1,32,128]{4,3,2,1,0:T(8,128)(2,1)S(1)}, bf16[1,16,1,32,128]{4,3,2,1,0:T(8,128)(2,1)S(1)}, u32[]{:S(2)}, u32[]{:S(2)}) collective-permute-start(bf16[1,16,1,32,128]{4,3,2,1,0:T(8,128)(2,1)S(1)} %get-tuple-element.50), channel_id=1, source_target_pairs={{4,0},{8,4},{12,8},{5,1},{9,5},{13,9},{6,2},{10,6},{14,10},{7,3},{... | collective-permute-start | bytes 393224 | tf_op jit(solution)/shard_map/ppermute | solution.py:18
  58.6 1.0 copy-start.5
  61.9 1.0 copy-start.8
  61.9 1.0 copy-start.11
  115.1 7.3 %collective-permute-start.4 = (bf16[1,16,1,32,128]{4,3,2,1,0:T(8,128)(2,1)}, bf16[1,16,1,32,128]{4,3,2,1,0:T(8,128)(2,1)S(1)}, u32[]{:S(2)}, u32[]{:S(2)}) collective-permute-start(bf16[1,16,1,32,128]{4,3,2,1,0:T(8,128)(2,1)} %get-tuple-element.45), channel_id=1, source_target_pairs={{0,4},{4,8},{8,12},{1,5},{5,9},{9,13},{2,6},{6,10},{10,14},{3,7},{... | collective-permute-start | bytes 393224 | tf_op jit(solution)/shard_map/ppermute | solution.py:16
  117.3 7.1 %collective-permute-start.5 = (bf16[1,16,1,32,128]{4,3,2,1,0:T(8,128)(2,1)}, bf16[1,16,1,32,128]{4,3,2,1,0:T(8,128)(2,1)S(1)}, u32[]{:S(2)}, u32[]{:S(2)}) collective-permute-start(bf16[1,16,1,32,128]{4,3,2,1,0:T(8,128)(2,1)} %get-tuple-element.46), channel_id=1, source_target_pairs={{4,0},{8,4},{12,8},{5,1},{9,5},{13,9},{6,2},{10,6},{14,10},{7,3},{... | collective-permute-start | bytes 393224 | tf_op jit(solution)/shard_map/ppermute | solution.py:18
  147.3 7.9 %copy-start.2 = (bf16[1,16,4,32,128]{4,3,2,1,0:T(8,128)(2,1)S(1)}, bf16[1,16,4,32,128]{4,3,2,1,0:T(8,128)(2,1)}, u32[]{:S(2)}) copy-start(bf16[1,16,4,32,128]{4,3,2,1,0:T(8,128)(2,1)} %copy-done.1) | copy-start | bytes 1572868
  153.3 2.3 copy-start.4
  160.5 25.3 %copy-start.9 = (f32[1,128,128]{2,1,0:T(8,128)S(1)}, f32[1,128,128]{2,1,0:T(8,128)}, u32[]{:S(2)}) copy-start(f32[1,128,128]{2,1,0:T(8,128)} %convolution_bitcast_fusion.14) | copy-start | bytes 196612
  183.2 5.9 %collective-permute-start.6 = (bf16[1,16,1,32,128]{4,3,2,1,0:T(8,128)(2,1)S(1)}, bf16[1,16,1,32,128]{4,3,2,1,0:T(8,128)(2,1)S(1)}, u32[]{:S(2)}, u32[]{:S(2)}) collective-permute-start(bf16[1,16,1,32,128]{4,3,2,1,0:T(8,128)(2,1)S(1)} %get-tuple-element.41), channel_id=1, source_target_pairs={{0,4},{4,8},{8,12},{1,5},{5,9},{9,13},{2,6},{6,10},{10,14},{3,7},{... | collective-permute-start | bytes 393224 | tf_op jit(solution)/shard_map/ppermute | solution.py:16
  184.5 7.6 %collective-permute-start.7 = (bf16[1,16,1,32,128]{4,3,2,1,0:T(8,128)(2,1)S(1)}, bf16[1,16,1,32,128]{4,3,2,1,0:T(8,128)(2,1)S(1)}, u32[]{:S(2)}, u32[]{:S(2)}) collective-permute-start(bf16[1,16,1,32,128]{4,3,2,1,0:T(8,128)(2,1)S(1)} %get-tuple-element.42), channel_id=1, source_target_pairs={{4,0},{8,4},{12,8},{5,1},{9,5},{13,9},{6,2},{10,6},{14,10},{7,3},{... | collective-permute-start | bytes 393224 | tf_op jit(solution)/shard_map/ppermute | solution.py:18
  192.6 1.0 copy-start.7
Sparse Core Ops, SparseCore 0:
  188.6 130.3 all-reduce.6
